TPU v7x, 32 devices: a whole 2x2x4 slice. The times are simulated.
32 devices in a mesh: frame: 16 (over z, y, core), rec: 2 (over x).
Axes of the slice: x: 2, y: 2, z: 4, core: 2. Of those that a mesh axis runs over, the one named last changes fastest.
Arguments:
- code_indices: int32 [2, 4096, 8], P('rec', 'frame'), may hold values from 0 to 7
- lengths: int32 [2], P('rec'), may hold values from 2048 to 4096
- cotangent: bfloat16 [2, 1310720], P('rec', 'frame'), may hold values from -6 to 6
- embed_weight: float32 [8, 512], replicated, may hold values from -2 to 2
- embed_bias: float32 [512], replicated, may hold values from -3 to 3
- depth_kernel: float32 [7, 512], replicated, may hold values from -2 to 2
- depth_bias: float32 [512], replicated, may hold values from -3 to 3
- norm_gain: float32 [512], replicated, may hold values from 0.5 to 1.5
- norm_bias: float32 [512], replicated, may hold values from -1.75 to 1.75
- up_weight: bfloat16 [512, 1536], replicated, may hold values from -0.25 to 0.25
- up_bias: float32 [1536], replicated, may hold values from -3 to 3
- down_weight: bfloat16 [1536, 512], replicated, may hold values from -0.15625 to 0.15625
- down_bias: float32 [512], replicated, may hold values from -1.75 to 1.75
- layer_scale: float32 [512], replicated, may hold values from 0.3 to 1
- head_weight: bfloat16 [512, 1280], replicated, may hold values from -0.25 to 0.25
- head_bias: float32 [1280], replicated, may hold values from -3 to 3
Outputs:
- embed_weight_grad: float32 [8, 512], P(None, 'frame')
- embed_bias_grad: float32 [512], P('frame')
- depth_kernel_grad: float32 [7, 512], P(None, 'frame')
- depth_bias_grad: float32 [512], P('frame')
- norm_gain_grad: float32 [512], P('frame')
- norm_bias_grad: float32 [512], P('frame')
- up_weight_grad: float32 [512, 1536], P('frame')
- up_bias_grad: float32 [1536], P('frame')
- down_weight_grad: float32 [1536, 512], P('frame')
- down_bias_grad: float32 [512], P('frame')
- layer_scale_grad: float32 [512], P('frame')
- head_weight_grad: float32 [512, 1280], P('frame')
- head_bias_grad: float32 [1280], P('frame')
Inputs may be any that keep to these rules, and one draw needn't show every extreme that they name: `lengths`: frames at or after a recording's length are padding.
All inputs are finite; a program needn't handle non-finite values.
Results may differ from a plain program's by a relative error of at most 0.011.
Values may be sent and summed in bfloat16 or wider, within the bound.
A program may use at most 64 MiB of HBM per device.

v0:
```python
import jax
import jax.numpy as jnp
from jax import lax
from jax.sharding import PartitionSpec as P

LEVELS = 8
KERNEL = 7
NFFT = 1280
HOP = 320
BINS = 640
PAD = 480


EPSILON = 1e-06


def padded_2(block, sides, width):
    for axis, dim in sides:
        count = lax.axis_size(axis)
        forward = [(i, i + 1) for i in range(count - 1)]
        backward = [(target, source) for source, target in forward]
        low = lax.ppermute(
            lax.slice_in_dim(block, block.shape[dim] - width, None, axis=dim), axis, forward
        )
        high = lax.ppermute(lax.slice_in_dim(block, 0, width, axis=dim), axis, backward)
        block = jnp.concatenate([low, block, high], axis=dim)
    return block


def hann_square(position, fft_size):
    window = 0.5 - 0.5 * jnp.cos(2.0 * jnp.pi / fft_size * position)
    return window * window


def synthesis(fft_size, bin_count):
    sample = jnp.arange(fft_size, dtype=jnp.int32)[:, None]
    frequency = jnp.arange(bin_count, dtype=jnp.int32)[None, :]
    turn_count = (sample * frequency % fft_size).astype(jnp.float32)
    angles = 2.0 * jnp.pi / fft_size * turn_count
    window = 0.5 - 0.5 * jnp.cos(2.0 * jnp.pi / fft_size * sample.astype(jnp.float32))
    factor = jnp.where(frequency == 0, 1.0, 2.0).astype(jnp.float32) * window / fft_size
    real_part = factor * jnp.cos(angles)
    imag_part = jnp.where(frequency == 0, 0.0, -factor * jnp.sin(angles))
    return jnp.concatenate([real_part, imag_part], axis=1).astype(jnp.bfloat16)


def sample_scale(first_sample, sample_count, total_frames, hop_size, fft_size, length):
    pad_size = (fft_size - hop_size) // 2
    sample = first_sample + jnp.arange(sample_count, dtype=jnp.int32)
    block_id = sample // hop_size
    offset = sample - block_id * hop_size + pad_size
    envelope = jnp.zeros((sample_count,), jnp.float32)
    for step_back in range(-2, 3):
        frame_id = block_id - step_back
        inside = offset + step_back * hop_size
        usable = (frame_id >= 0) & (frame_id < total_frames) & (inside >= 0) & (inside < fft_size)
        square = hann_square(inside.astype(jnp.float32), fft_size)
        envelope = envelope + jnp.where(usable, square, 0.0)
    alive_mask = sample < length * hop_size
    return jnp.where(alive_mask, 1.0 / envelope, 0.0)


def layer_norm(conv_out, norm_gain, norm_bias):
    centre = conv_out - jnp.mean(conv_out, axis=-1, keepdims=True)
    spread = jnp.mean(centre * centre, axis=-1, keepdims=True)
    return centre * lax.rsqrt(spread + EPSILON) * norm_gain + norm_bias


def exact_gelu(hidden_pre):
    return jax.nn.gelu(hidden_pre, approximate=False)


def head_map(logits):
    bin_count = logits.shape[1] // 2
    magnitude = jnp.exp(logits[:, :bin_count])
    phase_angle = logits[:, bin_count:]
    return jnp.concatenate(
        [magnitude * jnp.cos(phase_angle), magnitude * jnp.sin(phase_angle)], axis=1
    )


def contract_rows(former, latter, precision=None):
    return lax.dot_general(
        former,
        latter,
        (((0,), (0,)), ((), ())),
        precision=precision,
        preferred_element_type=jnp.float32,
    )


def contract_cols(former, latter):
    return lax.dot_general(
        former, latter, (((1,), (1,)), ((), ())), preferred_element_type=jnp.float32
    )


def embed_rows(code_rows, valid_rows, embed_weight, embed_bias):
    levels_half = (LEVELS - 1) / 2.0
    values = (code_rows.astype(jnp.float32) - levels_half) / levels_half
    projected = jnp.dot(values, embed_weight, precision=lax.Precision.HIGHEST) + embed_bias
    return (values, (valid_rows[:, None] * projected).astype(jnp.bfloat16))


def body(
    code_indices,
    lengths,
    cotangent,
    embed_weight,
    embed_bias,
    depth_kernel,
    depth_bias,
    norm_gain,
    norm_bias,
    up_weight,
    up_bias,
    down_weight,
    down_bias,
    layer_scale,
    head_weight,
    head_bias,
):
    code_rows = code_indices[0]
    frame_count = code_rows.shape[0]
    total_frames = frame_count * lax.axis_size("frame")
    first_frame = lax.axis_index("frame") * frame_count
    length = lengths[0]
    frame_ids = first_frame + jnp.arange(frame_count, dtype=jnp.int32)
    valid = (frame_ids < length).astype(jnp.float32)
    values, features = embed_rows(code_rows, valid, embed_weight, embed_bias)
    rim_codes = padded_2(code_rows, (("frame", 0),), 3)
    edge_codes = jnp.concatenate([rim_codes[:3], rim_codes[frame_count + 3 :]], axis=0)
    edge_ids = jnp.concatenate(
        [
            first_frame - 3 + jnp.arange(3, dtype=jnp.int32),
            first_frame + frame_count + jnp.arange(3, dtype=jnp.int32),
        ]
    )
    edge_valid = ((edge_ids >= 0) & (edge_ids < total_frames) & (edge_ids < length)).astype(
        jnp.float32
    )
    edge_values, edge_features = embed_rows(edge_codes, edge_valid, embed_weight, embed_bias)
    padded = jnp.concatenate([edge_features[:3], features, edge_features[3:]], axis=0)
    conv_out = jnp.zeros((frame_count, features.shape[1]), jnp.float32) + depth_bias
    for tap_index in range(KERNEL):
        conv_out = conv_out + depth_kernel[tap_index] * padded[
            tap_index : tap_index + frame_count
        ].astype(jnp.float32)
    normed, norm_pullback = jax.vjp(layer_norm, conv_out, norm_gain, norm_bias)
    normed_low = normed.astype(jnp.bfloat16)
    hidden_pre = jnp.dot(normed_low, up_weight, preferred_element_type=jnp.float32) + up_bias
    activated, gelu_pullback = jax.vjp(exact_gelu, hidden_pre)
    activated_low = activated.astype(jnp.bfloat16)
    branch = jnp.dot(activated_low, down_weight, preferred_element_type=jnp.float32) + down_bias
    latent = (features.astype(jnp.float32) + layer_scale * branch).astype(jnp.bfloat16)
    logits = jnp.dot(latent, head_weight, preferred_element_type=jnp.float32) + head_bias
    spectrum, head_pullback = jax.vjp(head_map, logits)
    sample_weight = sample_scale(
        first_frame * HOP, frame_count * HOP, total_frames, HOP, NFFT, length
    )
    sample_grad = (cotangent[0].astype(jnp.float32) * sample_weight).astype(jnp.bfloat16)
    extended = padded_2(sample_grad, (("frame", 0),), PAD)
    hop_rows = extended.reshape(frame_count + 3, HOP)
    frame_grad = jnp.concatenate(
        [hop_rows[quarter : quarter + frame_count] for quarter in range(4)], axis=1
    )
    spec_grad = jnp.dot(frame_grad, synthesis(NFFT, BINS), preferred_element_type=jnp.float32)
    logit_grad = head_pullback(spec_grad)[0]
    logit_low = logit_grad.astype(jnp.bfloat16)
    head_weight_grad = contract_rows(latent, logit_low)
    head_bias_grad = jnp.sum(logit_grad, axis=0)
    latent_grad = contract_cols(logit_low, head_weight)
    layer_scale_grad = jnp.sum(latent_grad * branch, axis=0)
    branch_grad = layer_scale * latent_grad
    down_bias_grad = jnp.sum(branch_grad, axis=0)
    branch_low = branch_grad.astype(jnp.bfloat16)
    down_weight_grad = contract_rows(activated_low, branch_low)
    activated_grad = contract_cols(branch_low, down_weight)
    hidden_grad = gelu_pullback(activated_grad)[0]
    up_bias_grad = jnp.sum(hidden_grad, axis=0)
    hidden_low = hidden_grad.astype(jnp.bfloat16)
    up_weight_grad = contract_rows(normed_low, hidden_low)
    normed_grad = contract_cols(hidden_low, up_weight)
    conv_grad, norm_gain_grad, norm_bias_grad = norm_pullback(normed_grad)
    depth_kernel_grad = jnp.stack(
        [
            jnp.sum(
                conv_grad * padded[tap_index : tap_index + frame_count].astype(jnp.float32), axis=0
            )
            for tap_index in range(KERNEL)
        ],
        axis=0,
    )
    depth_bias_grad = jnp.sum(conv_grad, axis=0)
    conv_rims = padded_2(conv_grad.astype(jnp.bfloat16), (("frame", 0),), 3).astype(conv_grad.dtype)
    feature_grad = latent_grad
    for tap_index in range(KERNEL):
        feature_grad = (
            feature_grad
            + depth_kernel[tap_index] * conv_rims[6 - tap_index : 6 - tap_index + frame_count]
        )
    feature_grad = valid[:, None] * feature_grad
    embed_weight_grad = contract_rows(values, feature_grad, lax.Precision.HIGHEST)
    embed_bias_grad = jnp.sum(feature_grad, axis=0)
    shares = (
        lax.psum_scatter(embed_weight_grad, "frame", scatter_dimension=1, tiled=True),
        lax.psum_scatter(embed_bias_grad, "frame", scatter_dimension=0, tiled=True),
        lax.psum_scatter(depth_kernel_grad, "frame", scatter_dimension=1, tiled=True),
        lax.psum_scatter(depth_bias_grad, "frame", scatter_dimension=0, tiled=True),
        lax.psum_scatter(norm_gain_grad, "frame", scatter_dimension=0, tiled=True),
        lax.psum_scatter(norm_bias_grad, "frame", scatter_dimension=0, tiled=True),
        lax.psum_scatter(up_weight_grad, "frame", scatter_dimension=0, tiled=True),
        lax.psum_scatter(up_bias_grad, "frame", scatter_dimension=0, tiled=True),
        lax.psum_scatter(down_weight_grad, "frame", scatter_dimension=0, tiled=True),
        lax.psum_scatter(down_bias_grad, "frame", scatter_dimension=0, tiled=True),
        lax.psum_scatter(layer_scale_grad, "frame", scatter_dimension=0, tiled=True),
        lax.psum_scatter(head_weight_grad, "frame", scatter_dimension=0, tiled=True),
        lax.psum_scatter(head_bias_grad, "frame", scatter_dimension=0, tiled=True),
    )
    totals = lax.psum(
        (
            shares[0],
            shares[1],
            shares[2],
            shares[3],
            shares[4],
            shares[5],
            shares[6],
            shares[7],
            shares[8],
            shares[9],
            shares[10],
            shares[11],
            shares[12],
        ),
        "rec",
    )
    return (
        totals[0],
        totals[1],
        totals[2],
        totals[3],
        totals[4],
        totals[5],
        totals[6],
        totals[7],
        totals[8],
        totals[9],
        totals[10],
        totals[11],
        totals[12],
    )


def solution(mesh):
    return jax.shard_map(
        body,
        mesh=mesh,
        in_specs=(
            P("rec", "frame", None),
            P("rec"),
            P("rec", "frame"),
            P(),
            P(),
            P(),
            P(),
            P(),
            P(),
            P(),
            P(),
            P(),
            P(),
            P(),
            P(),
            P(),
        ),
        out_specs=(
            P(None, "frame"),
            P("frame"),
            P(None, "frame"),
            P("frame"),
            P("frame"),
            P("frame"),
            P("frame", None),
            P("frame"),
            P("frame", None),
            P("frame"),
            P("frame"),
            P("frame", None),
            P("frame"),
        ),
        check_vma=False,
    )
```

profile of v0, /device:TPU:0, one launch (start us, length us, event | category | flops | bytes accessed | tf_op | source)
XLA Modules:
  0.0 429.7 jit_solution(9328089790398117431)
XLA Ops:
  7.2 1.4 convert_element_type.151
  9.3 6.5 %multiply_convert_fusion.3 = bf16[81920]{0:T(1024)(128)(2,1)S(1)} fusion(f32[81920]{0:T(1024)S(1)} %bitcast.49, s32[]{:T(128)S(6)} %mul.451, s32[]{:T(128)S(6)} %mul.450), kind=kLoop, calls=%fused_computation.111 | loop fusion | flops 7700480 | bytes 491528 | tf_op jit(solution)/shard_map/convert_element_type | solution.py:161
  15.9 1.3 collective-permute-start.3
  17.2 3.0 collective-permute-start.2
  21.1 1.3 collective-permute-start.1
  22.4 5.1 %collective-permute-start = (s32[3,8]{1,0:T(4,128)S(1)}, s32[3,8]{1,0:T(4,128)S(1)}, u32[]{:S(2)}, u32[]{:S(2)}) collective-permute-start(s32[3,8]{1,0:T(4,128)S(1)} %bitcast.74), channel_id=1, source_target_pairs={{0,2},{2,4},{4,6},{6,8},{8,10},{10,12},{12,14},{14,16},{16,18},{18... | collective-permute-start | bytes 296 | tf_op jit(solution)/shard_map/ppermute | solution.py:22
  28.7 15.6 %multiply_convert_fusion = (bf16[1280,640]{1,0:T(8,128)(2,1)}, bf16[1280,640]{1,0:T(8,128)(2,1)}) fusion(f32[1280]{0:T(1024)S(1)} %multiply_subtract_fusion.1, f32[640]{0:T(1024)S(1)} %broadcast_select_fusion, pred[640]{0:T(1024)(128)(4,1)S(1)} %iota_compare_fusion), kind=kLoop, calls=%fused_computation.8 | loop fusion | flops 13926400 | bytes 3285120 | tf_op jit(solution)/shard_map/convert.1
  46.2 5.2 %multiply_convert_fusion.1 = (bf16[256,1536]{1,0:T(8,128)(2,1)S(1)}, f32[256,1536]{1,0:T(8,128)}, f32[256,1536]{1,0:T(8,128)}) fusion(f32[1536]{0:T(1024)S(1)} %copy-done.22, bf16[512,1536]{1,0:T(8,128)(2,1)S(1)} %copy-done, f32[256,512]{1,0:T(8,128)S(1)} %get-tuple-element.57, f32[512]{0:T(512)S(1)} %copy-done.19, f32[512]{0:T(512)S(1)} %copy-done.17, ...), kind=kOutput, calls=%fused_computation.19 | convolution fusion | flops 429260800 | bytes 6041600 | tf_op jit(solution)/shard_map/dot_general | solution.py:151
  51.4 1.4 fusion.34
  53.1 1.6 convolution_add_fusion
  57.0 3.2 fusion.2
  60.3 2.6 multiply_add_fusion.1
  62.9 2.0 fusion.70
  65.2 2.0 fusion.72
  67.5 2.4 fusion.109
  70.8 2.4 fusion.44
  73.2 3.6 fusion.68
  77.0 1.9 multiply_reduce_fusion.1
  81.2 1.3 collective-permute-start.5
  82.4 4.3 %collective-permute-start.4 = (bf16[3,512]{1,0:T(4,128)(2,1)S(1)}, bf16[3,512]{1,0:T(4,128)(2,1)S(1)}, u32[]{:S(2)}, u32[]{:S(2)}) collective-permute-start(bf16[3,512]{1,0:T(4,128)(2,1)S(1)} %get-tuple-element.63), channel_id=1, source_target_pairs={{0,2},{2,4},{4,6},{6,8},{8,10},{10,12},{12,14},{14,16},{16,18},{18... | collective-permute-start | bytes 9224 | tf_op jit(solution)/shard_map/ppermute | solution.py:22
  88.8 1.6 multiply_reduce_fusion
  90.5 1.7 convolution_bitcast_fusion
  92.2 40.5 %reduce-scatter.14.cloned.1.call-done = f32[32,1280]{1,0:T(8,128)} async-done(((f32[512,1280]{1,0:T(8,128)}), f32[32,1280]{1,0:T(8,128)}) %reduce-scatter.14.cloned.1.call-update) | async-done | bytes 163856 | tf_op jit(solution)/shard_map/reduce_scatter | solution.py:217
  132.7 69.1 %reduce-scatter.10.cloned.1.call-done = f32[32,1536]{1,0:T(8,128)} async-done(((f32[512,1536]{1,0:T(8,128)}), f32[32,1536]{1,0:T(8,128)}) %reduce-scatter.10.cloned.1.call-update) | async-done | bytes 196624 | tf_op jit(solution)/shard_map/reduce_scatter | solution.py:212
  201.8 69.1 %reduce-scatter.12.cloned.1.call-done = f32[96,512]{1,0:T(8,128)} async-done(((f32[1536,512]{1,0:T(8,128)}), f32[96,512]{1,0:T(8,128)}) %reduce-scatter.12.cloned.1.call-update) | async-done | bytes 196624 | tf_op jit(solution)/shard_map/reduce_scatter | solution.py:214
  273.6 57.7 %all-reduce.10 = (f32[512]{0:T(512)S(1)}, f32[512]{0:T(512)S(1)}, f32[512]{0:T(512)S(1)}, f32[512]{0:T(512)S(1)}, f32[1536]{0:T(1024)S(1)}, /*index=5*/f32[512]{0:T(512)S(1)}, f32[512]{0:T(512)S(1)}, f32[1280]{0:T(1024)S(1)}) all-reduce(f32[512]{0:T(512)S(1)} %get-tuple-element.61, ...), channel_id=3, replica_groups=mesh['frame'=16,'rec'=2] {'frame'}, use_global_device_ids=true, to_apply=%region_7.8.clone | all-reduce | flops 5888 | bytes 47104
  332.7 54.6 %reduce-scatter.16.cloned.1.call-done = f32[32,8]{1,0:T(8,128)} async-done(((f32[512,8]{1,0:T(8,128)}), f32[32,8]{1,0:T(8,128)}) %reduce-scatter.16.cloned.1.call-update) | async-done | bytes 1040
  388.0 8.7 %all-reduce.11 = (f32[8,32]{1,0:T(8,128)}, f32[32]{0:T(128)}, f32[7,32]{1,0:T(8,128)}, f32[32]{0:T(128)}, f32[32]{0:T(128)}, /*index=5*/f32[32]{0:T(128)}, f32[9...) all-reduce(f32[8,32]{1,0:T(8,128)S(1)} %copy.36, ...), channel_id=1, replica_groups=mesh['frame'=16,'rec'=2] {'rec'}, use_global_device_ids=true, to_apply=%region_5.6 | all-reduce | flops 848 | bytes 6784 | tf_op jit(solution)/shard_map/psum | solution.py:220
  396.7 21.3 %all-reduce.15.cloned.1.call-done = (f32[32,1536]{1,0:T(8,128)}, f32[96,512]{1,0:T(8,128)}, f32[32,1280]{1,0:T(8,128)}) async-done(((f32[32,1536]{1,0:T(8,128)}, f32[96,512]{1,0:T(8,128)}, f32[32,1280]{1,0:T(8,128)}), (f32[32,1536]{1,0:T(8,128)}, f32[96,512]{1,0:T(8,128)}, f32[32,1280]{1,0:T(8,128)})) %all-reduce.15.cloned.1.call-update) | async-done | bytes 557072 | tf_op jit(solution)/shard_map/psum | solution.py:220
  418.0 1.6 copy.43
  419.6 1.6 copy.44
  421.2 1.6 copy.45
  (115 shorter events, 15.1 us)
Async XLA Ops:
  7.2 38.9 %copy-start = (bf16[512,1536]{1,0:T(8,128)(2,1)S(1)}, bf16[512,1536]{1,0:T(8,128)(2,1)}, u32[]{:S(2)}) copy-start(bf16[512,1536]{1,0:T(8,128)(2,1)} %param.25) | copy-start | bytes 4718596
  7.2 125.5 %reduce-scatter.14.cloned.1.call-start = ((), (), s32[]{:S(2)}) async-start(), calls=%async_computation.7 | async-start | bytes 2785280 | tf_op jit(solution)/shard_map/reduce_scatter | solution.py:217
  15.9 38.8 %collective-permute-start.3 = (bf16[480]{0:T(512)(128)(2,1)S(1)}, bf16[480]{0:T(512)(128)(2,1)S(1)}, u32[]{:S(2)}, u32[]{:S(2)}) collective-permute-start(bf16[480]{0:T(512)(128)(2,1)S(1)} %get-tuple-element.71), channel_id=1, source_target_pairs={{2,0},{4,2},{6,4},{8,6},{10,8},{12,10},{14,12},{16,14},{18,16},{20... | collective-permute-start | bytes 2888 | tf_op jit(solution)/shard_map/ppermute | solution.py:25
  17.2 37.5 %collective-permute-start.2 = (bf16[480]{0:T(512)(128)(2,1)S(1)}, bf16[480]{0:T(512)(128)(2,1)S(1)}, u32[]{:S(2)}, u32[]{:S(2)}) collective-permute-start(bf16[480]{0:T(512)(128)(2,1)S(1)} %get-tuple-element.72), channel_id=1, source_target_pairs={{0,2},{2,4},{4,6},{6,8},{8,10},{10,12},{12,14},{14,16},{16,18},{18... | collective-permute-start | bytes 2888 | tf_op jit(solution)/shard_map/ppermute | solution.py:22
  21.1 24.1 %collective-permute-start.1 = (s32[3,8]{1,0:T(4,128)S(1)}, s32[3,8]{1,0:T(4,128)S(1)}, u32[]{:S(2)}, u32[]{:S(2)}) collective-permute-start(s32[3,8]{1,0:T(4,128)S(1)} %bitcast.73), channel_id=1, source_target_pairs={{2,0},{4,2},{6,4},{8,6},{10,8},{12,10},{14,12},{16,14},{18,16},{20... | collective-permute-start | bytes 296 | tf_op jit(solution)/shard_map/ppermute | solution.py:25
  22.4 22.7 %collective-permute-start = (s32[3,8]{1,0:T(4,128)S(1)}, s32[3,8]{1,0:T(4,128)S(1)}, u32[]{:S(2)}, u32[]{:S(2)}) collective-permute-start(s32[3,8]{1,0:T(4,128)S(1)} %bitcast.74), channel_id=1, source_target_pairs={{0,2},{2,4},{4,6},{6,8},{8,10},{10,12},{12,14},{14,16},{16,18},{18... | collective-permute-start | bytes 296 | tf_op jit(solution)/shard_map/ppermute | solution.py:22
  28.7 15.7 %copy-start.14 = (s32[1,256,8]{1,2,0:T(8,128)S(1)}, s32[1,256,8]{1,2,0:T(8,128)}, u32[]{:S(2)}) copy-start(s32[1,256,8]{1,2,0:T(8,128)} %param.16) | copy-start | bytes 24580
  28.7 15.7 %copy-start.21 = (f32[8,512]{1,0:T(8,128)S(1)}, f32[8,512]{1,0:T(8,128)}, u32[]{:S(2)}) copy-start(f32[8,512]{1,0:T(8,128)} %param.19) | copy-start | bytes 49156
  28.7 15.7 %copy-start.23 = (f32[512]{0:T(512)S(1)}, f32[512]{0:T(512)}, u32[]{:S(2)}) copy-start(f32[512]{0:T(512)} %param.20) | copy-start | bytes 6148
  28.7 16.6 %copy-start.18 = (f32[512]{0:T(512)S(1)}, f32[512]{0:T(512)}, u32[]{:S(2)}) copy-start(f32[512]{0:T(512)} %param.22) | copy-start | bytes 6148
  44.4 1.8 copy-start.17
  44.4 1.8 copy-start.19
  44.4 1.8 copy-start.22
  45.0 6.3 %copy-start.6 = (bf16[256,512]{1,0:T(8,128)(2,1)}, bf16[256,512]{1,0:T(8,128)(2,1)S(1)}, u32[]{:S(2)}) copy-start(bf16[256,512]{1,0:T(8,128)(2,1)S(1)} %fusion.16) | copy-start | bytes 786436
  46.2 5.2 %copy-start.10 = (bf16[1536,512]{1,0:T(8,128)(2,1)S(1)}, bf16[1536,512]{1,0:T(8,128)(2,1)}, u32[]{:S(2)}) copy-start(bf16[1536,512]{1,0:T(8,128)(2,1)} %param.27) | copy-start | bytes 4718596
  46.2 5.2 %copy-start.15 = (f32[512]{0:T(512)S(1)}, f32[512]{0:T(512)}, u32[]{:S(2)}) copy-start(f32[512]{0:T(512)} %param.29) | copy-start | bytes 6148
  46.2 5.2 %copy-start.20 = (f32[512]{0:T(512)S(1)}, f32[512]{0:T(512)}, u32[]{:S(2)}) copy-start(f32[512]{0:T(512)} %param.28) | copy-start | bytes 6148
  52.8 2.2 copy-start.8
  57.0 3.3 copy-start.2
  60.3 2.6 copy-start.9
  64.9 136.9 %reduce-scatter.10.cloned.1.call-start = ((), (), s32[]{:S(2)}) async-start(), calls=%async_computation.5 | async-start | bytes 3342336 | tf_op jit(solution)/shard_map/reduce_scatter | solution.py:212
  65.2 2.0 copy-start.11
  65.2 2.3 copy-start.25
  67.2 2.7 copy-start.3
  73.2 197.7 %reduce-scatter.12.cloned.1.call-start = ((), (), s32[]{:S(2)}) async-start(), calls=%async_computation.6 | async-start | bytes 3342336 | tf_op jit(solution)/shard_map/reduce_scatter | solution.py:214
  76.9 255.0 %reduce-scatter.18.cloned.1.call-start = ((), (), s32[]{:S(2)}) async-start(), calls=%async_computation.9 | async-start | bytes 278528
  79.1 9.7 %copy-start.4 = (f32[256,512]{1,0:T(8,128)S(1)}, f32[256,512]{1,0:T(8,128)}, u32[]{:S(2)}) copy-start(f32[256,512]{1,0:T(8,128)} %copy-done.3) | copy-start | bytes 1572868
  81.2 6.6 %collective-permute-start.5 = (bf16[3,512]{1,0:T(4,128)(2,1)S(1)}, bf16[3,512]{1,0:T(4,128)(2,1)S(1)}, u32[]{:S(2)}, u32[]{:S(2)}) collective-permute-start(bf16[3,512]{1,0:T(4,128)(2,1)S(1)} %get-tuple-element.64), channel_id=1, source_target_pairs={{2,0},{4,2},{6,4},{8,6},{10,8},{12,10},{14,12},{16,14},{18,16},{20... | collective-permute-start | bytes 9224 | tf_op jit(solution)/shard_map/ppermute | solution.py:25
  82.4 5.3 %collective-permute-start.4 = (bf16[3,512]{1,0:T(4,128)(2,1)S(1)}, bf16[3,512]{1,0:T(4,128)(2,1)S(1)}, u32[]{:S(2)}, u32[]{:S(2)}) collective-permute-start(bf16[3,512]{1,0:T(4,128)(2,1)S(1)} %get-tuple-element.63), channel_id=1, source_target_pairs={{0,2},{2,4},{4,6},{6,8},{8,10},{10,12},{12,14},{14,16},{16,18},{18... | collective-permute-start | bytes 9224 | tf_op jit(solution)/shard_map/ppermute | solution.py:22
  87.7 299.5 %reduce-scatter.16.cloned.1.call-start = ((), (), s32[]{:S(2)}) async-start(), calls=%async_computation.8 | async-start | bytes 278528
  90.4 180.5 %copy-start.24 = (u32[32]{0:T(128)S(1)}, u32[32]{0:T(128)}, u32[]{:S(2)}) copy-start(u32[32]{0:T(128)} %constant.168) | copy-start | bytes 388
  92.2 325.8 %all-reduce.15.cloned.1.call-start = ((), (), s32[]{:S(2)}) async-start(), calls=%async_computation.10 | async-start | bytes 1114112 | tf_op jit(solution)/shard_map/psum | solution.py:220
  (6 other events, 7.4 us)
Sparse Core Ops, SparseCore 0:
  65.1 67.5 reduce-scatter.13
  136.5 65.2 reduce-scatter.9
  205.6 65.2 reduce-scatter.11
  274.3 54.7 reduce-scatter.17
  332.5 54.7 reduce-scatter.15
  389.5 28.4 all-reduce.14
where the time goes:
time: 431 us; the launch traced here: 430 us
  waiting for transfers between devices  255 us (59%)
  blocking collectives  66.4 us (15%)
  other arithmetic  31 us (7%)
  matrix products  28.1 us (7%)
  between operations  17.3 us (4%)
  starting transfers between devices  16.8 us (4%)
  local copies, waits for them, and re-layouts  15.4 us (4%)
    reduce_scatter x1, waiting for transfers between devices, body(): lax.psum_scatter(down_weight_grad, 'frame', scatter_dimension=0, tiled=True)  69.1 us
    reduce_scatter x1, waiting for transfers between devices, body(): lax.psum_scatter(up_weight_grad, 'frame', scatter_dimension=0, tiled=True)  69.1 us
    unnamed x1, blocking collectives  57.7 us
    unnamed x8, waiting for transfers between devices  54.7 us
    reduce_scatter x1, waiting for transfers between devices, body(): lax.psum_scatter(head_weight_grad, 'frame', scatter_dimension=0, tiled=True)  40.5 us
    psum x1, waiting for transfers between devices, body(): lax.psum((shares[0], shares[1], shares[2], shares[3], shares[4], shares[5...  21.3 us
    another operation x1, other arithmetic  15.6 us
    ppermute x3, starting transfers between devices, padded_2(): lax.ppermute(lax.slice_in_dim(block, block.shape[dim] - width, None, axis...  12.5 us
  transfers between devices with their start and end apart: 12, of which 5 were waited for; matrix products, arithmetic and copies ran while one was open for 11% of the time, Pallas kernels for 0%

commit v1 on v0

--- a/solution.py
+++ b/solution.py
@@ -1,6 +1,8 @@
 import jax
 import jax.numpy as jnp
 from jax import lax
+from jax.experimental import pallas as pl
+from jax.experimental.pallas import tpu as pltpu
 from jax.sharding import PartitionSpec as P
 
 LEVELS = 8
@@ -33,15 +35,31 @@
 
 
 def synthesis(fft_size, bin_count):
-    sample = jnp.arange(fft_size, dtype=jnp.int32)[:, None]
+    fine_count = 40
     frequency = jnp.arange(bin_count, dtype=jnp.int32)[None, :]
-    turn_count = (sample * frequency % fft_size).astype(jnp.float32)
-    angles = 2.0 * jnp.pi / fft_size * turn_count
-    window = 0.5 - 0.5 * jnp.cos(2.0 * jnp.pi / fft_size * sample.astype(jnp.float32))
-    factor = jnp.where(frequency == 0, 1.0, 2.0).astype(jnp.float32) * window / fft_size
-    real_part = factor * jnp.cos(angles)
-    imag_part = jnp.where(frequency == 0, 0.0, -factor * jnp.sin(angles))
-    return jnp.concatenate([real_part, imag_part], axis=1).astype(jnp.bfloat16)
+
+    def turns(sample):
+        angle = (2.0 * jnp.pi / fft_size) * (sample * frequency % fft_size).astype(jnp.float32)
+        return lax.optimization_barrier((jnp.cos(angle), jnp.sin(angle)))
+
+    coarse_cos, coarse_sin = turns(
+        jnp.arange(0, fft_size, fine_count, dtype=jnp.int32)[:, None]
+    )
+    fine_cos, fine_sin = turns(jnp.arange(fine_count, dtype=jnp.int32)[:, None])
+    sample = jnp.arange(fft_size, dtype=jnp.float32)
+    window = lax.optimization_barrier(
+        (0.5 - 0.5 * jnp.cos(2.0 * jnp.pi / fft_size * sample)) / fft_size
+    ).reshape(fft_size // fine_count, fine_count, 1)
+    factor = window * jnp.where(frequency == 0, 1.0, 2.0)[None]
+    cc, cs = coarse_cos[:, None, :], coarse_sin[:, None, :]
+    fc, fs = fine_cos[None], fine_sin[None]
+    real_part = factor * (cc * fc - cs * fs)
+    imag_part = jnp.where(frequency[None] == 0, 0.0, -factor * (cs * fc + cc * fs))
+    shape = (fft_size, bin_count)
+    return (
+        real_part.astype(jnp.bfloat16).reshape(shape),
+        imag_part.astype(jnp.bfloat16).reshape(shape),
+    )
 
 
 def sample_scale(first_sample, sample_count, total_frames, hop_size, fft_size, length):
@@ -100,6 +118,190 @@
     values = (code_rows.astype(jnp.float32) - levels_half) / levels_half
     projected = jnp.dot(values, embed_weight, precision=lax.Precision.HIGHEST) + embed_bias
     return (values, (valid_rows[:, None] * projected).astype(jnp.bfloat16))
+
+
+def reduce_kernel(chips, recs, arrays, *refs):
+    groups = [refs[i * arrays : (i + 1) * arrays] for i in range(7)]
+    ins, outs, pair_in, pair_sum, chip_in, final, final_in = groups
+    pair_send, pair_recv, chip_send, chip_recv, rec_send, rec_recv = refs[7 * arrays :]
+    total = chips * recs
+    frame, rec = lax.axis_index("frame"), lax.axis_index("rec")
+    core = lax.rem(frame, 2)
+    chip = lax.div(frame, 2)
+    me = rec * chips + chip
+    partner = frame + 1 - 2 * core
+
+    def place(step):
+        target = lax.rem(me + step, total)
+        return lax.rem(target, chips), lax.div(target, chips)
+
+    def pair_copy(i, step):
+        j, h = place(step)
+        return pltpu.make_async_remote_copy(
+            src_ref=ins[i].at[j, 1 - core, h],
+            dst_ref=pair_in[i].at[j, h],
+            send_sem=pair_send.at[i, step],
+            recv_sem=pair_recv.at[i, step],
+            device_id={"rec": rec, "frame": partner},
+            device_id_type=pl.DeviceIdType.MESH,
+        )
+
+    def chip_copy(i, step):
+        j, h = place(step)
+        return pltpu.make_async_remote_copy(
+            src_ref=pair_sum[i].at[j, h],
+            dst_ref=chip_in[i].at[step],
+            send_sem=chip_send.at[i, step],
+            recv_sem=chip_recv.at[i, step],
+            device_id={"rec": h, "frame": 2 * j + core},
+            device_id_type=pl.DeviceIdType.MESH,
+        )
+
+    def rec_copy(i, step):
+        return pltpu.make_async_remote_copy(
+            src_ref=final[i],
+            dst_ref=final_in[i].at[step],
+            send_sem=rec_send.at[i, step],
+            recv_sem=rec_recv.at[i, step],
+            device_id={"rec": lax.rem(rec + step, recs), "frame": frame},
+            device_id_type=pl.DeviceIdType.MESH,
+        )
+
+    barrier = pltpu.get_barrier_semaphore()
+    pl.semaphore_signal(
+        barrier,
+        inc=1,
+        device_id={"rec": rec, "frame": partner},
+        device_id_type=pl.DeviceIdType.MESH,
+    )
+
+    @pl.loop(1, total)
+    def _(step):
+        j, h = place(step)
+        pl.semaphore_signal(
+            barrier,
+            inc=1,
+            device_id={"rec": h, "frame": 2 * j + core},
+            device_id_type=pl.DeviceIdType.MESH,
+        )
+
+    pl.semaphore_wait(barrier, total)
+
+    for i in range(arrays):
+
+        @pl.loop(1, total)
+        def _(step):
+            pair_copy(i, step).start()
+
+        pair_copy(i, 0).start()
+
+    for i in range(arrays):
+
+        @pl.loop(1, total)
+        def _(step):
+            j, h = place(step)
+            pair_copy(i, step).wait_recv()
+            pair_sum[i][j, h] = (
+                ins[i][j, core, h].astype(jnp.float32) + pair_in[i][j, h].astype(jnp.float32)
+            ).astype(pair_sum[i].dtype)
+            chip_copy(i, step).start()
+
+    for i in range(arrays):
+        pair_copy(i, 0).wait_recv()
+        own = ins[i][chip, core, rec].astype(jnp.float32) + pair_in[i][chip, rec].astype(
+            jnp.float32
+        )
+
+        def add(step, value):
+            chip_copy(i, step).wait_recv()
+            return value + chip_in[i][step].astype(jnp.float32)
+
+        value = lax.fori_loop(1, total, add, own).astype(final[i].dtype)
+        final[i][...] = value
+        for step in range(1, recs):
+            rec_copy(i, step).start()
+        outs[i][rec] = value.astype(jnp.float32)
+
+    for i in range(arrays):
+        for step in range(1, recs):
+            rec_copy(i, step).wait_recv()
+            outs[i][lax.rem(rec + recs - step, recs)] = final_in[i][step].astype(jnp.float32)
+
+    for i in range(arrays):
+        for step in range(1, recs):
+            rec_copy(i, step).wait_send()
+        pair_copy(i, 0).wait_send()
+
+        @pl.loop(1, total)
+        def _(step):
+            pair_copy(i, step).wait_send()
+            chip_copy(i, step).wait_send()
+
+
+def reduce_all(parts, chips, recs):
+    arrays, total = len(parts), chips * recs
+    scratch = [pltpu.VMEM((chips, recs) + part.shape[3:], part.dtype) for part in parts] * 2
+    scratch += [pltpu.VMEM((total,) + part.shape[3:], part.dtype) for part in parts]
+    scratch += [pltpu.VMEM(part.shape[3:], part.dtype) for part in parts]
+    scratch += [pltpu.VMEM((recs,) + part.shape[3:], part.dtype) for part in parts]
+    scratch += [pltpu.SemaphoreType.DMA((arrays, total))] * 4
+    scratch += [pltpu.SemaphoreType.DMA((arrays, recs))] * 2
+    return pl.pallas_call(
+        lambda *refs: reduce_kernel(chips, recs, arrays, *refs),
+        name="reduce_all",
+        out_shape=[jax.ShapeDtypeStruct(part.shape[2:], jnp.float32) for part in parts],
+        in_specs=[pl.BlockSpec(memory_space=pltpu.VMEM)] * arrays,
+        out_specs=[pl.BlockSpec(memory_space=pltpu.VMEM)] * arrays,
+        scratch_shapes=scratch,
+        compiler_params=pltpu.CompilerParams(
+            collective_id=0, has_side_effects=True, vmem_limit_bytes=48 * 1024 * 1024
+        ),
+    )(*parts)
+
+
+def shared_sum(grads):
+    frames, recs = lax.axis_size("frame"), lax.axis_size("rec")
+    split = (1, 0, 1, 0, 0, 0, 0, 0, 0, 0, 0, 0, 0)
+    large = [11, 8, 6]
+    rows = [grads[k].shape[0] // (frames * recs) for k in large]
+    if frames % 2 or any(count == 0 or count % 16 for count in rows):
+        shares = tuple(
+            lax.psum_scatter(grad.astype(jnp.float32), "frame", scatter_dimension=dim, tiled=True)
+            for grad, dim in zip(grads, split)
+        )
+        return lax.psum(shares, "rec")
+    chips = frames // 2
+    parts = [
+        grads[k].astype(jnp.bfloat16).reshape(chips, 2, recs, count, grads[k].shape[1])
+        for k, count in zip(large, rows)
+    ]
+    small = [k for k in range(len(grads)) if k not in large]
+    pieces, shapes = [], []
+    for k in small:
+        grad = grads[k]
+        if split[k]:
+            piece = grad.reshape(grad.shape[0], frames, -1).transpose(1, 0, 2)
+            shapes.append(piece.shape[1:])
+            piece = piece.reshape(frames, -1)
+        else:
+            piece = grad.reshape(frames, -1)
+            shapes.append(piece.shape[1:])
+        pieces.append(piece)
+    widths = [piece.shape[1] for piece in pieces]
+    used = sum(widths)
+    unit = 8 * 128 * recs
+    padded = -(-used // unit) * unit
+    packed = jnp.concatenate(pieces + [jnp.zeros((frames, padded - used), jnp.float32)], axis=1)
+    parts.append(packed.reshape(chips, 2, recs, padded // (128 * recs), 128))
+    sums = reduce_all(parts, chips, recs)
+    out = [None] * len(grads)
+    for k, total in zip(large, sums):
+        out[k] = total.reshape(-1, total.shape[2])
+    flat, start = sums[-1].reshape(-1), 0
+    for k, width, shape in zip(small, widths, shapes):
+        out[k] = flat[start : start + width].reshape(shape)
+        start += width
+    return tuple(out)
 
 
 def body(
@@ -164,7 +366,14 @@
     frame_grad = jnp.concatenate(
         [hop_rows[quarter : quarter + frame_count] for quarter in range(4)], axis=1
     )
-    spec_grad = jnp.dot(frame_grad, synthesis(NFFT, BINS), preferred_element_type=jnp.float32)
+    real_table, imag_table = synthesis(NFFT, BINS)
+    spec_grad = jnp.concatenate(
+        [
+            jnp.dot(frame_grad, real_table, preferred_element_type=jnp.float32),
+            jnp.dot(frame_grad, imag_table, preferred_element_type=jnp.float32),
+        ],
+        axis=1,
+    )
     logit_grad = head_pullback(spec_grad)[0]
     logit_low = logit_grad.astype(jnp.bfloat16)
     head_weight_grad = contract_rows(latent, logit_low)
@@ -202,53 +411,22 @@
     feature_grad = valid[:, None] * feature_grad
     embed_weight_grad = contract_rows(values, feature_grad, lax.Precision.HIGHEST)
     embed_bias_grad = jnp.sum(feature_grad, axis=0)
-    shares = (
-        lax.psum_scatter(embed_weight_grad, "frame", scatter_dimension=1, tiled=True),
-        lax.psum_scatter(embed_bias_grad, "frame", scatter_dimension=0, tiled=True),
-        lax.psum_scatter(depth_kernel_grad, "frame", scatter_dimension=1, tiled=True),
-        lax.psum_scatter(depth_bias_grad, "frame", scatter_dimension=0, tiled=True),
-        lax.psum_scatter(norm_gain_grad, "frame", scatter_dimension=0, tiled=True),
-        lax.psum_scatter(norm_bias_grad, "frame", scatter_dimension=0, tiled=True),
-        lax.psum_scatter(up_weight_grad, "frame", scatter_dimension=0, tiled=True),
-        lax.psum_scatter(up_bias_grad, "frame", scatter_dimension=0, tiled=True),
-        lax.psum_scatter(down_weight_grad, "frame", scatter_dimension=0, tiled=True),
-        lax.psum_scatter(down_bias_grad, "frame", scatter_dimension=0, tiled=True),
-        lax.psum_scatter(layer_scale_grad, "frame", scatter_dimension=0, tiled=True),
-        lax.psum_scatter(head_weight_grad, "frame", scatter_dimension=0, tiled=True),
-        lax.psum_scatter(head_bias_grad, "frame", scatter_dimension=0, tiled=True),
-    )
-    totals = lax.psum(
+    return shared_sum(
         (
-            shares[0],
-            shares[1],
-            shares[2],
-            shares[3],
-            shares[4],
-            shares[5],
-            shares[6],
-            shares[7],
-            shares[8],
-            shares[9],
-            shares[10],
-            shares[11],
-            shares[12],
-        ),
-        "rec",
-    )
-    return (
-        totals[0],
-        totals[1],
-        totals[2],
-        totals[3],
-        totals[4],
-        totals[5],
-        totals[6],
-        totals[7],
-        totals[8],
-        totals[9],
-        totals[10],
-        totals[11],
-        totals[12],
+            embed_weight_grad,
+            embed_bias_grad,
+            depth_kernel_grad,
+            depth_bias_grad,
+            norm_gain_grad,
+            norm_bias_grad,
+            up_weight_grad,
+            up_bias_grad,
+            down_weight_grad,
+            down_bias_grad,
+            layer_scale_grad,
+            head_weight_grad,
+            head_bias_grad,
+        )
     )
 
 

time: 431 us -> 159 us (0.37)
  waiting for transfers between devices: 255 us -> 0.02 us
  Pallas kernels: 0 us -> 67.6 us
  blocking collectives: 66.4 us -> 0 us
  between operations: 17.3 us -> 1.92 us
  other arithmetic: 31 us -> 19.3 us
  local copies, waits for them, and re-layouts: 15.4 us -> 26.9 us
    reduce_scatter x3 -> x0, waiting for transfers between devices: 179 us -> none  [the longest x1 69.1 us: body(): lax.psum_scatter(down_weight_grad, 'frame', scatter_dimension=0, tiled=True)]
    pallas_call x0 -> x1, Pallas kernels: none -> 67.6 us  [reduce_all(): pl.pallas_call(lambda *refs: reduce_kernel(chips, recs, arrays, *refs), n...]
    unnamed x1 -> x0, blocking collectives: 57.7 us -> none
    unnamed x8 -> x0, waiting for transfers between devices: 54.7 us -> none
    psum x1 -> x0, waiting for transfers between devices: 21.3 us -> none  [body(): lax.psum((shares[0], shares[1], shares[2], shares[3], shares[4], shares[5...]
    another operation x1 -> x0, other arithmetic: 15.6 us -> none
    psum x1 -> x0, blocking collectives: 8.71 us -> none  [body(): lax.psum((shares[0], shares[1], shares[2], shares[3], shares[4], shares[5...]
    slice x4, local copies, waits for them, and re-layouts: 0.76 us -> 7.17 us  [body(): hop_rows[quarter:quarter + frame_count]]
  transfers between devices with their start and end apart: 12 -> 6, of which waited for: 5 -> 0; matrix products, arithmetic and copies ran while one was open for 11% -> 16% of each run, Pallas kernels for 0% -> 0%
where the time goes in v1:
time: 159 us; the launch traced here: 158 us
  Pallas kernels  67.6 us (43%)
  local copies, waits for them, and re-layouts  26.9 us (17%)
  matrix products  25.9 us (16%)
  other arithmetic  19.3 us (12%)
  starting transfers between devices  16.3 us (10%)
  between operations  1.92 us (1%)
    pallas_call x1, Pallas kernels, reduce_all(): pl.pallas_call(lambda *refs: reduce_kernel(chips, recs, arrays, *refs), n...  67.6 us
    ppermute x3, starting transfers between devices, padded_2(): lax.ppermute(lax.slice_in_dim(block, block.shape[dim] - width, None, axis...  12.4 us
    unnamed x76, local copies, waits for them, and re-layouts  8.6 us
    slice x4, local copies, waits for them, and re-layouts, body(): hop_rows[quarter:quarter + frame_count]  7.17 us
    convert_element_type x1, other arithmetic, body(): (cotangent[0].astype(jnp.float32) * sample_weight).astype(jnp.bfloat16)  6.47 us
    dot_general x4, matrix products, contract_rows(): lax.dot_general(former, latter, (((0,), (0,)), ((), ())), precision=preci...  6.29 us
    dot_general x1, matrix products, body(): jnp.dot(normed_low, up_weight, preferred_element_type=jnp.float32) + up_bias  5.32 us
    dot_general x1, matrix products, body(): jnp.dot(frame_grad, real_table, preferred_element_type=jnp.float32)  5.14 us
  transfers between devices with their start and end apart: 6, of which 0 were waited for; matrix products, arithmetic and copies ran while one was open for 16% of the time, Pallas kernels for 0%

profile of v1, /device:TPU:0, one launch (start us, length us, event | category | flops | bytes accessed | tf_op | source)
XLA Modules:
  0.0 157.8 jit_solution(9579675062712373489)
XLA Ops:
  1.7 1.3 collective-permute-start.1
  3.0 3.6 %collective-permute-start = (s32[3,8]{1,0:T(4,128)S(1)}, s32[3,8]{1,0:T(4,128)}, u32[]{:S(2)}, u32[]{:S(2)}) collective-permute-start(s32[3,8]{1,0:T(4,128)S(1)} %bitcast.88), channel_id=1, source_target_pairs={{0,2},{2,4},{4,6},{6,8},{8,10},{10,12},{12,14},{14,16},{16,18},{18... | collective-permute-start | bytes 296 | tf_op jit(solution)/shard_map/ppermute | solution.py:24
  7.3 1.3 convert_element_type.168
  8.6 6.5 %multiply_convert_fusion.2 = bf16[81920]{0:T(1024)(128)(2,1)S(1)} fusion(f32[81920]{0:T(1024)S(1)} %bitcast.71, s32[]{:T(128)S(6)} %mul.526, s32[]{:T(128)S(6)} %mul.525), kind=kLoop, calls=%fused_computation.107 | loop fusion | flops 7700480 | bytes 491528 | tf_op jit(solution)/shard_map/convert_element_type | solution.py:363
  15.7 1.3 collective-permute-start.3
  17.0 5.2 %collective-permute-start.2 = (bf16[480]{0:T(512)(128)(2,1)}, bf16[480]{0:T(512)(128)(2,1)}, u32[]{:S(2)}, u32[]{:S(2)}) collective-permute-start(bf16[480]{0:T(512)(128)(2,1)} %get-tuple-element.69), channel_id=1, source_target_pairs={{0,2},{2,4},{4,6},{6,8},{8,10},{10,12},{12,14},{14,16},{16,18},{18... | collective-permute-start | bytes 2888 | tf_op jit(solution)/shard_map/ppermute | solution.py:24
  25.2 1.9 %fusion.2 = (bf16[1280,640]{1,0:T(8,128)(2,1)S(1)}, bf16[1280,640]{1,0:T(8,128)(2,1)}) fusion(f32[32,40,640]{2,1,0:T(8,128)S(1)} %get-tuple-element.58, f32[640]{0:T(1024)S(1)} %broadcast_select_fusion, f32[1280]{0:T(1024)S(1)} %subtract_multiply_fusion, pred[640]{0:T(1024)(128)(4,1)S(1)} %copy-done.28, f32[32,40,640]{2,1,0:T(8,128)S(1)} %get-tuple-element.59), kind=kLoop, calls=%fused_computation.4 | loop fusion | flops 5734400 | bytes 9838720 | tf_op jit(solution)/shard_map/convert_element_type | solution.py:61
  28.9 5.3 %multiply_convert_fusion = (bf16[256,1536]{1,0:T(8,128)(2,1)S(1)}, f32[256,1536]{1,0:T(8,128)}, f32[256,1536]{1,0:T(8,128)}) fusion(f32[1536]{0:T(1024)S(1)} %copy-done.31, bf16[512,1536]{1,0:T(8,128)(2,1)S(1)} %copy-done, f32[256,512]{1,0:T(8,128)S(1)} %get-tuple-element.52, f32[512]{0:T(512)S(1)} %copy-done.26, f32[512]{0:T(512)S(1)} %copy-done.24, ...), kind=kOutput, calls=%fused_computation.16 | convolution fusion | flops 429260800 | bytes 6041600 | tf_op jit(solution)/shard_map/dot_general | solution.py:353
  34.3 1.4 fusion.29
  36.0 1.6 %convolution_add_fusion = f32[256,1280]{1,0:T(8,128)} fusion(bf16[256,512]{1,0:T(8,128)(2,1)S(1)} %get-tuple-element.92, bf16[512,1280]{1,0:T(8,128)(2,1)S(1)} %copy-done.6, f32[1280]{0:T(1024)S(1)} %copy-done.23), kind=kOutput, calls=%fused_computation.11 | convolution fusion | flops 335872000 | bytes 2888704 | tf_op jit(solution)/shard_map/dot_general | solution.py:358
  37.6 1.9 %pad_maximum_fusion.2 = (bf16[81920]{0:T(1024)(128)(2,1)}, bf16[81920]{0:T(1024)(128)(2,1)}, bf16[81920]{0:T(1024)(128)(2,1)}, bf16[81920]{0:T(1024)(128)(2,1)}) fusion(bf16[480]{0:T(512)(128)(2,1)} %collective-permute-done.3, bf16[81920]{0:T(1024)(128)(2,1)S(1)} %copy-done.19, bf16[480]{0:T(512)(128)(2,1)} %collective-permute-done.2), kind=kLoop, calls=%fused_computation.143 | loop fusion | flops 1310720 | bytes 821120 | tf_op jit(solution)/shard_map/concatenate | solution.py:28
  39.5 1.8 %slice.207 = bf16[256,320]{1,0:T(8,128)(2,1)} reshape(bf16[81920]{0:T(1024)(128)(2,1)} %get-tuple-element.66) | data formatting | bytes 327680 | tf_op jit(solution)/shard_map/slice | solution.py:367
  41.3 1.8 %slice.209 = bf16[256,320]{1,0:T(8,128)(2,1)} reshape(bf16[81920]{0:T(1024)(128)(2,1)} %get-tuple-element.67) | data formatting | bytes 327680 | tf_op jit(solution)/shard_map/slice | solution.py:367
  43.1 1.8 %slice.212 = bf16[256,320]{1,0:T(8,128)(2,1)} reshape(bf16[81920]{0:T(1024)(128)(2,1)} %get-tuple-element.63) | data formatting | bytes 327680 | tf_op jit(solution)/shard_map/slice | solution.py:367
  44.9 1.8 %slice.214 = bf16[256,320]{1,0:T(8,128)(2,1)} reshape(bf16[81920]{0:T(1024)(128)(2,1)} %get-tuple-element.62) | data formatting | bytes 327680 | tf_op jit(solution)/shard_map/slice | solution.py:367
  46.7 2.1 %concatenate.52 = bf16[256,1280]{1,0:T(8,128)(2,1)} concatenate(bf16[256,320]{1,0:T(8,128)(2,1)} %slice.207, bf16[256,320]{1,0:T(8,128)(2,1)} %slice.209, bf16[256,320]{1,0:T(8,128)(2,1)} %slice.212, bf16[256,320]{1,0:T(8,128)(2,1)} %slice.214), dimensions={1} | concatenate | bytes 1310720 | tf_op jit(solution)/shard_map/concatenate | solution.py:366
  48.8 1.9 %fusion.116 = f32[256,640]{1,0:T(8,128)S(1)} fusion(bf16[256,1280]{1,0:T(8,128)(2,1)} %concatenate.52, bf16[1280,640]{1,0:T(8,128)(2,1)S(1)} %get-tuple-element.77), kind=kOutput, calls=%fused_computation.211 | convolution fusion | flops 419430400 | bytes 2949120 | tf_op jit(solution)/shard_map/dot_general | solution.py:373
  50.8 5.1 %multiply_add_fusion.2 = (f32[256,640]{1,0:T(8,128)S(1)}, f32[256,640]{1,0:T(8,128)S(1)}) fusion(f32[256,640]{1,0:T(8,128)S(1)} %fusion.116, f32[256,1280]{1,0:T(8,128)} %convolution_add_fusion, bf16[256,1280]{1,0:T(8,128)(2,1)S(1)} %copy-done.11, bf16[1280,640]{1,0:T(8,128)(2,1)S(1)} %copy-done.14), kind=kOutput, calls=%fused_computation.59 | convolution fusion | flops 421068800 | bytes 5570560 | tf_op jit(solution)/shard_map/dot_general | solution.py:372
  55.9 1.6 %convolution_convert_fusion.2 = bf16[512,1280]{1,0:T(8,128)(2,1)} fusion(bf16[256,512]{1,0:T(8,128)(2,1)S(1)} %copy-done.13, f32[256,640]{1,0:T(8,128)S(1)} %get-tuple-element.54, f32[256,640]{1,0:T(8,128)S(1)} %get-tuple-element.53), kind=kOutput, calls=%fused_computation.10 | convolution fusion | flops 336855040 | bytes 2883584 | tf_op jit(solution)/shard_map/dot_general | solution.py:101
  60.6 1.0 fusion.115
  61.6 1.9 %convolution_convert_fusion = bf16[512,1536]{1,0:T(8,128)(2,1)} fusion(bf16[256,1536]{1,0:T(8,128)(2,1)S(1)} %get-tuple-element.96, f32[256,512]{1,0:T(8,128)S(1)} %copy-done.5, f32[512]{0:T(512)S(1)} %copy-done.26, f32[512]{0:T(512)S(1)} %copy-done.24, f32[256]{0:T(256)S(1)} %fusion.93, f32[256]{0:T(256)S(1)} %broadcast_multiply_fusion), kind=kOutput, calls=%fused_computation.8 | convolution fusion | flops 404094976 | bytes 2889728 | tf_op jit(solution)/shard_map/dot_general | solution.py:101
  63.5 1.2 multiply_reduce_fusion.1
  65.7 1.3 collective-permute-start.5
  67.0 3.7 %collective-permute-start.4 = (bf16[3,512]{1,0:T(4,128)(2,1)S(1)}, bf16[3,512]{1,0:T(4,128)(2,1)S(1)}, u32[]{:S(2)}, u32[]{:S(2)}) collective-permute-start(bf16[3,512]{1,0:T(4,128)(2,1)S(1)} %get-tuple-element.60), channel_id=1, source_target_pairs={{0,2},{2,4},{4,6},{6,8},{8,10},{10,12},{12,14},{14,16},{16,18},{18... | collective-permute-start | bytes 9224 | tf_op jit(solution)/shard_map/ppermute | solution.py:24
  72.7 1.0 maximum_convert_fusion
  73.7 2.6 %multiply_reduce_fusion = (f32[512]{0:T(512)S(1)}, f32[512]{0:T(512)S(1)}, f32[512]{0:T(512)S(1)}, f32[256,512]{1,0:T(8,128)}) fusion(f32[256,512]{1,0:T(8,128)} %copy-done.8, f32[256,512]{1,0:T(8,128)} %get-tuple-element.93, f32[512]{0:T(512)S(1)} %copy-done.21, f32[262,512]{1,0:T(8,128)S(1)} %maximum_convert_fusion, f32[512]{0:T(512)S(1)} %bitcast.84, ...), kind=kLoop, calls=%fused_computation.92 | loop fusion | flops 2619904 | bytes 5266432 | tf_op jit(solution)/shard_map/reduce_sum | solution.py:382
  76.3 2.0 %copy.34 = f32[512,256]{1,0:T(8,128)} copy(f32[512,256]{0,1:T(8,128)} %bitcast.68) | data formatting | bytes 1048576 | tf_op jit(solution)/shard_map/dot_general | solution.py:101
  78.3 2.2 %convolution_bitcast_fusion = f32[16,8,32]{2,1,0:T(8,128)S(1)} fusion(f32[16,32,256]{2,1,0:T(8,128)} %bitcast.69, s32[1,256,8]{1,2,0:T(8,128)S(1)} %copy-done.20), kind=kOutput, calls=%fused_computation.35 | convolution fusion | flops 12589056 | bytes 548864 | tf_op jit(solution)/shard_map/dot_general | solution.py:101
  81.0 1.4 copy-done.1
  82.4 1.3 copy-done.2
  83.7 67.6 %reduce_all.1 = (f32[2,16,1280]{2,1,0:T(8,128)S(1)}, f32[2,48,512]{2,1,0:T(8,128)S(1)}, f32[2,16,1536]{2,1,0:T(8,128)S(1)}, f32[2,8,128]{2,1,0:T(8,128)S(1)}) custom-call(bf16[8,2,2,16,1280]{4,3,2,1,0:T(8,128)(2,1)S(1)} %bitcast.60, bf16[8,2,2,48,512]{4,3,2,1,0:T(8,128)(2,1)S(1)} %bitcast.58, bf16[8,2,2,16,1536]{4,3,2,1,0:T(8,128)(2,1)S(1)} %bitcast.59, ...), custom_call_target="tpu_custom_call" | custom-call | tf_op jit(solution)/shard_map/reduce_all/pallas_call | solution.py:249
  156.2 1.6 %copy.42 = f32[32,1280]{1,0:T(8,128)} copy(f32[32,1280]{1,0:T(8,128)} %bitcast.64) | data formatting | bytes 327680
  (135 shorter events, 17.9 us)
Async XLA Ops:
  0.6 28.2 %copy-start = (bf16[512,1536]{1,0:T(8,128)(2,1)S(1)}, bf16[512,1536]{1,0:T(8,128)(2,1)}, u32[]{:S(2)}) copy-start(bf16[512,1536]{1,0:T(8,128)(2,1)} %param.25) | copy-start | bytes 4718596
  0.7 23.0 %copy-start.20 = (s32[1,256,8]{1,2,0:T(8,128)S(1)}, s32[1,256,8]{1,2,0:T(8,128)}, u32[]{:S(2)}) copy-start(s32[1,256,8]{1,2,0:T(8,128)} %param.16) | copy-start | bytes 24580
  0.7 22.6 %copy-start.22 = (f32[7,512]{1,0:T(8,128)S(1)}, f32[7,512]{1,0:T(8,128)}, u32[]{:S(2)}) copy-start(f32[7,512]{1,0:T(8,128)} %param.21) | copy-start | bytes 43012
  0.7 23.0 %copy-start.29 = (f32[8,512]{1,0:T(8,128)S(1)}, f32[8,512]{1,0:T(8,128)}, u32[]{:S(2)}) copy-start(f32[8,512]{1,0:T(8,128)} %param.19) | copy-start | bytes 49156
  0.7 23.0 %copy-start.32 = (f32[512]{0:T(512)S(1)}, f32[512]{0:T(512)}, u32[]{:S(2)}) copy-start(f32[512]{0:T(512)} %param.20) | copy-start | bytes 6148
  1.7 25.5 %collective-permute-start.1 = (s32[3,8]{1,0:T(4,128)S(1)}, s32[3,8]{1,0:T(4,128)}, u32[]{:S(2)}, u32[]{:S(2)}) collective-permute-start(s32[3,8]{1,0:T(4,128)S(1)} %bitcast.87), channel_id=1, source_target_pairs={{2,0},{4,2},{6,4},{8,6},{10,8},{12,10},{14,12},{16,14},{18,16},{20... | collective-permute-start | bytes 296 | tf_op jit(solution)/shard_map/ppermute | solution.py:27
  3.0 24.1 %collective-permute-start = (s32[3,8]{1,0:T(4,128)S(1)}, s32[3,8]{1,0:T(4,128)}, u32[]{:S(2)}, u32[]{:S(2)}) collective-permute-start(s32[3,8]{1,0:T(4,128)S(1)} %bitcast.88), channel_id=1, source_target_pairs={{0,2},{2,4},{4,6},{6,8},{8,10},{10,12},{12,14},{14,16},{16,18},{18... | collective-permute-start | bytes 296 | tf_op jit(solution)/shard_map/ppermute | solution.py:24
  15.1 1.9 %copy-start.18 = (bf16[81920]{0:T(1024)(128)(2,1)}, bf16[81920]{0:T(1024)(128)(2,1)S(1)}, u32[]{:S(2)}) copy-start(bf16[81920]{0:T(1024)(128)(2,1)S(1)} %multiply_convert_fusion.2) | copy-start | bytes 491524
  15.7 21.9 %collective-permute-start.3 = (bf16[480]{0:T(512)(128)(2,1)}, bf16[480]{0:T(512)(128)(2,1)}, u32[]{:S(2)}, u32[]{:S(2)}) collective-permute-start(bf16[480]{0:T(512)(128)(2,1)} %get-tuple-element.68), channel_id=1, source_target_pairs={{2,0},{4,2},{6,4},{8,6},{10,8},{12,10},{14,12},{16,14},{18,16},{20... | collective-permute-start | bytes 2888 | tf_op jit(solution)/shard_map/ppermute | solution.py:27
  17.0 20.6 %collective-permute-start.2 = (bf16[480]{0:T(512)(128)(2,1)}, bf16[480]{0:T(512)(128)(2,1)}, u32[]{:S(2)}, u32[]{:S(2)}) collective-permute-start(bf16[480]{0:T(512)(128)(2,1)} %get-tuple-element.69), channel_id=1, source_target_pairs={{0,2},{2,4},{4,6},{6,8},{8,10},{10,12},{12,14},{14,16},{16,18},{18... | collective-permute-start | bytes 2888 | tf_op jit(solution)/shard_map/ppermute | solution.py:24
  25.1 2.1 %copy-start.30 = (f32[8,512]{1,0:T(8,128)S(1)}, f32[8,512]{1,0:T(8,128)}, u32[]{:S(2)}) copy-start(f32[8,512]{1,0:T(8,128)} %param.19) | copy-start | bytes 49156
  25.1 2.1 %copy-start.33 = (f32[512]{0:T(512)S(1)}, f32[512]{0:T(512)}, u32[]{:S(2)}) copy-start(f32[512]{0:T(512)} %param.20) | copy-start | bytes 6148
  25.1 2.9 %copy-start.25 = (f32[512]{0:T(512)S(1)}, f32[512]{0:T(512)}, u32[]{:S(2)}) copy-start(f32[512]{0:T(512)} %param.22) | copy-start | bytes 6148
  25.1 3.7 %copy-start.24 = (f32[512]{0:T(512)S(1)}, f32[512]{0:T(512)}, u32[]{:S(2)}) copy-start(f32[512]{0:T(512)} %param.23) | copy-start | bytes 6148
  25.1 3.7 %copy-start.26 = (f32[512]{0:T(512)S(1)}, f32[512]{0:T(512)}, u32[]{:S(2)}) copy-start(f32[512]{0:T(512)} %param.24) | copy-start | bytes 6148
  25.2 3.7 %copy-start.31 = (f32[1536]{0:T(1024)S(1)}, f32[1536]{0:T(1024)}, u32[]{:S(2)}) copy-start(f32[1536]{0:T(1024)} %param.26) | copy-start | bytes 18436
  28.6 5.6 %copy-start.4 = (f32[256,512]{1,0:T(8,128)}, f32[256,512]{1,0:T(8,128)S(1)}, u32[]{:S(2)}) copy-start(f32[256,512]{1,0:T(8,128)S(1)} %get-tuple-element.52) | copy-start | bytes 1572868
  28.9 5.4 %copy-start.15 = (bf16[1536,512]{1,0:T(8,128)(2,1)S(1)}, bf16[1536,512]{1,0:T(8,128)(2,1)}, u32[]{:S(2)}) copy-start(bf16[1536,512]{1,0:T(8,128)(2,1)} %param.27) | copy-start | bytes 4718596
  28.9 5.4 %copy-start.21 = (f32[512]{0:T(512)S(1)}, f32[512]{0:T(512)}, u32[]{:S(2)}) copy-start(f32[512]{0:T(512)} %param.29) | copy-start | bytes 6148
  28.9 5.4 %copy-start.27 = (f32[512]{0:T(512)S(1)}, f32[512]{0:T(512)}, u32[]{:S(2)}) copy-start(f32[512]{0:T(512)} %param.28) | copy-start | bytes 6148
  35.7 3.8 %copy-start.12 = (bf16[256,512]{1,0:T(8,128)(2,1)}, bf16[256,512]{1,0:T(8,128)(2,1)S(1)}, u32[]{:S(2)}) copy-start(bf16[256,512]{1,0:T(8,128)(2,1)S(1)} %get-tuple-element.92) | copy-start | bytes 786436
  35.7 1.9 %copy-start.19 = (bf16[81920]{0:T(1024)(128)(2,1)S(1)}, bf16[81920]{0:T(1024)(128)(2,1)}, u32[]{:S(2)}) copy-start(bf16[81920]{0:T(1024)(128)(2,1)} %copy-done.18) | copy-start | bytes 491524
  48.8 1.9 %copy-start.11 = (bf16[256,1280]{1,0:T(8,128)(2,1)S(1)}, bf16[256,1280]{1,0:T(8,128)(2,1)}, u32[]{:S(2)}) copy-start(bf16[256,1280]{1,0:T(8,128)(2,1)} %concatenate.52) | copy-start | bytes 1966084
  48.8 1.9 %copy-start.14 = (bf16[1280,640]{1,0:T(8,128)(2,1)S(1)}, bf16[1280,640]{1,0:T(8,128)(2,1)}, u32[]{:S(2)}) copy-start(bf16[1280,640]{1,0:T(8,128)(2,1)} %get-tuple-element.78) | copy-start | bytes 4915204
  50.8 5.2 %copy-start.13 = (bf16[256,512]{1,0:T(8,128)(2,1)S(1)}, bf16[256,512]{1,0:T(8,128)(2,1)}, u32[]{:S(2)}) copy-start(bf16[256,512]{1,0:T(8,128)(2,1)} %copy-done.12) | copy-start | bytes 786436
  57.6 1.8 %copy-start.34 = (f32[256,1536]{1,0:T(8,128)S(1)}, f32[256,1536]{1,0:T(8,128)}, u32[]{:S(2)}) copy-start(f32[256,1536]{1,0:T(8,128)} %get-tuple-element.50) | copy-start | bytes 4718596
  57.6 2.2 %copy-start.35 = (f32[256,1536]{1,0:T(8,128)S(1)}, f32[256,1536]{1,0:T(8,128)}, u32[]{:S(2)}) copy-start(f32[256,1536]{1,0:T(8,128)} %get-tuple-element.91) | copy-start | bytes 4718596
  58.7 2.9 %copy-start.8 = (f32[256,512]{1,0:T(8,128)}, f32[256,512]{1,0:T(8,128)S(1)}, u32[]{:S(2)}) copy-start(f32[256,512]{1,0:T(8,128)S(1)} %fusion.70) | copy-start | bytes 1572868
  58.7 1.8 %copy-start.16 = (bf16[1536,512]{1,0:T(8,128)(2,1)S(1)}, bf16[1536,512]{1,0:T(8,128)(2,1)}, u32[]{:S(2)}) copy-start(bf16[1536,512]{1,0:T(8,128)(2,1)} %param.27) | copy-start | bytes 4718596
  65.6 5.1 %copy-start.17 = (bf16[256,512]{1,0:T(8,128)(2,1)}, bf16[256,512]{1,0:T(8,128)(2,1)S(1)}, u32[]{:S(2)}) copy-start(bf16[256,512]{1,0:T(8,128)(2,1)S(1)} %get-tuple-element.55) | copy-start | bytes 786436
  65.7 7.0 %collective-permute-start.5 = (bf16[3,512]{1,0:T(4,128)(2,1)S(1)}, bf16[3,512]{1,0:T(4,128)(2,1)S(1)}, u32[]{:S(2)}, u32[]{:S(2)}) collective-permute-start(bf16[3,512]{1,0:T(4,128)(2,1)S(1)} %get-tuple-element.61), channel_id=1, source_target_pairs={{2,0},{4,2},{6,4},{8,6},{10,8},{12,10},{14,12},{16,14},{18,16},{20... | collective-permute-start | bytes 9224 | tf_op jit(solution)/shard_map/ppermute | solution.py:27
  67.0 5.7 %collective-permute-start.4 = (bf16[3,512]{1,0:T(4,128)(2,1)S(1)}, bf16[3,512]{1,0:T(4,128)(2,1)S(1)}, u32[]{:S(2)}, u32[]{:S(2)}) collective-permute-start(bf16[3,512]{1,0:T(4,128)(2,1)S(1)} %get-tuple-element.60), channel_id=1, source_target_pairs={{0,2},{2,4},{4,6},{6,8},{8,10},{10,12},{12,14},{14,16},{16,18},{18... | collective-permute-start | bytes 9224 | tf_op jit(solution)/shard_map/ppermute | solution.py:24
  (10 other events, 12.8 us)
